TPU v7x, 512 devices: a whole 4x8x8 slice. The times are simulated.
512 devices in a mesh: feed: 32 (over x, z), chan: 8 (over y), tm: 2 (over core).
Axes of the slice: x: 4, y: 8, z: 8, core: 2. Of those that a mesh axis runs over, the one named last changes fastest.
Arguments:
- voltages: bfloat16 [2, 512, 32, 2, 4096], P(None, 'tm', 'chan', None, 'feed'), may hold values from -6 to 6
- beam_refs: bfloat16 [2, 2, 32, 8, 32, 2, 32, 512], P(None, 'tm', 'feed', None, 'chan'), may hold values from -3 to 3
- beam_weight: float32 [32, 512], replicated, may hold values from 0.25 to 4
- delays: float32 [2, 4096], P(None, 'feed'), may hold values from -3 to 3
- band_phase: float32 [2, 16], replicated, may hold values from -4 to 4
- rfi_flags: int32 [512, 32], P('tm', 'chan'), may hold values 0 or 1
- grid_rows: int32 [256], replicated, may hold values from 0 to 255, each once
Outputs:
- delay_grad: float32 [2, 4096], P(None, 'feed')
- band_grad: float32 [2, 16], replicated
Inputs may be any that keep to these rules, and one draw needn't show every extreme that they name: `grid_rows`: every row 0 to 255 is taken by exactly one feed position, the same for every cylinder.
All inputs are finite; a program needn't handle non-finite values. No bound on the sum of `rfi_flags` on one device may be relied on, other than what follows from the above.
Results may differ from a plain program's by a relative error of at most 0.017.
Values may be sent and summed in bfloat16 or wider, within the bound.
A program may use at most 128 MiB of HBM per device.

v0:
```python
import math

import jax
import jax.numpy as jnp
from jax import lax
from jax.sharding import PartitionSpec as P

CYL = 16
NSF = 256
EWB = 32
NSB = 512
BANDS = 16


full_turn = 2.0 * math.pi


def in_blocks(shard, dim, devices):
    before, after = (shard.shape[:dim], shard.shape[dim + 1 :])
    return jnp.moveaxis(shard.reshape(*before, devices, -1, *after), dim, 0)


def summed_on_arrival(shard, axis, dim):
    devices = lax.axis_size(axis)
    blocks = lax.all_to_all(in_blocks(shard, dim, devices), axis, 0, 0, tiled=True)
    return jnp.sum(blocks.astype(jnp.float32), axis=0)


def copy_for_each(shard, axis):
    copies = jnp.broadcast_to(shard, (lax.axis_size(axis), *shard.shape))
    return lax.all_to_all(copies, axis, split_axis=0, concat_axis=0, tiled=True)


def taken_together(shard, axis):
    everything = copy_for_each(shard, axis)
    return jnp.sum(everything, axis=0)


def in_one(arrays, axis):
    line, at, outs = (jnp.concatenate([a.reshape(-1) for a in arrays]), 0, [])
    subtotal = taken_together(line, axis)
    for a in arrays:
        outs.append(subtotal[at : at + a.size].reshape(a.shape))
        at += a.size
    return tuple(outs)


def dft_tables(grid_rows):
    cyl_index = jnp.arange(CYL, dtype=jnp.int32)
    east_index = jnp.arange(EWB, dtype=jnp.int32)
    east_angle = (
        full_turn / EWB * (east_index[:, None] * cyl_index[None, :] % EWB).astype(jnp.float32)
    )
    north_index = jnp.arange(NSB, dtype=jnp.int32)
    north_angle = (
        full_turn / NSB * (north_index[:, None] * grid_rows[None, :] % NSB).astype(jnp.float32)
    )
    east_real = (jnp.cos(east_angle) / math.sqrt(EWB)).astype(jnp.bfloat16)
    east_imag = (-jnp.sin(east_angle) / math.sqrt(EWB)).astype(jnp.bfloat16)
    north_real = (jnp.cos(north_angle) / math.sqrt(NSB)).astype(jnp.bfloat16)
    north_imag = (-jnp.sin(north_angle) / math.sqrt(NSB)).astype(jnp.bfloat16)
    east_forward = jnp.stack(
        [jnp.stack([east_real.T, east_imag.T], 1), jnp.stack([-east_imag.T, east_real.T], 1)], 0
    )
    north_forward = jnp.stack(
        [jnp.stack([north_real.T, north_imag.T], 1), jnp.stack([-north_imag.T, north_real.T], 1)], 0
    )
    east_adjoint = jnp.stack(
        [jnp.stack([east_real, -east_imag], 1), jnp.stack([east_imag, east_real], 1)], 0
    )
    north_adjoint = jnp.stack(
        [jnp.stack([north_real, -north_imag], 1), jnp.stack([north_imag, north_real], 1)], 0
    )
    return (east_forward, north_forward, north_adjoint, east_adjoint)


def band_basis(chan_index, chans_total):
    term_index = jnp.arange(BANDS).astype(jnp.float32)
    return math.sqrt(2.0 / chans_total) * jnp.cos(
        math.pi * (chan_index[:, None] + 0.5) * term_index[None, :] / chans_total
    )


def shards(voltages, beam_refs, beam_weight, delays, band_phase, rfi_flags, grid_rows):
    local_times = voltages.shape[1]
    local_chans = voltages.shape[2]
    pol_count = voltages.shape[3]
    times_total = local_times * lax.axis_size("tm")
    chans_total = local_chans * lax.axis_size("chan")
    east_forward, north_forward, north_adjoint, east_adjoint = dft_tables(grid_rows)
    chan_index = (
        lax.axis_index("chan") * local_chans + jnp.arange(local_chans, dtype=jnp.int32)
    ).astype(jnp.float32)
    frequency = 0.4 + 0.4 * (chan_index + 0.5) / chans_total
    basis = band_basis(chan_index, chans_total)
    offset = jnp.dot(band_phase, basis.T, precision=lax.Precision.HIGHEST)
    phases = full_turn * frequency[None, :, None] * delays[:, None, :] + offset[:, :, None]
    gain_real = jnp.transpose(jnp.cos(phases), (1, 0, 2))[None]
    gain_imag = jnp.transpose(-jnp.sin(phases), (1, 0, 2))[None]
    volt_real = voltages[0].astype(jnp.float32)
    volt_imag = voltages[1].astype(jnp.float32)
    gained = jnp.stack(
        [
            gain_real * volt_real - gain_imag * volt_imag,
            gain_real * volt_imag + gain_imag * volt_real,
        ]
    ).astype(jnp.bfloat16)
    exchanged = lax.all_to_all(gained, "feed", split_axis=1, concat_axis=4, tiled=True)
    block_times = exchanged.shape[1]
    row_count = block_times * local_chans * pol_count
    row_start = lax.axis_index("feed") * block_times
    flags_rows = lax.dynamic_slice_in_dim(rfi_flags, row_start, block_times, 0)
    keep_weight = (1 - flags_rows).astype(jnp.float32) / times_total
    keep_weight = jnp.broadcast_to(
        keep_weight[:, :, None], (block_times, local_chans, pol_count)
    ).reshape(row_count)
    sectioned = exchanged.reshape(2, row_count, NSF, CYL)
    east_beams = jnp.einsum(
        "arnc,acbe->bren", sectioned, east_forward, preferred_element_type=jnp.float32
    ).astype(jnp.bfloat16)
    beam_field = jnp.einsum(
        "aren,anbm->brem", east_beams, north_forward, preferred_element_type=jnp.float32
    )
    ref_field = beam_refs.reshape(2, row_count, EWB, NSB).astype(jnp.float32)
    residual = (
        keep_weight[None, :, None, None] * beam_weight[None, None] * (beam_field - ref_field)
    ).astype(jnp.bfloat16)
    north_back = jnp.einsum(
        "brem,bman->aren", residual, north_adjoint, preferred_element_type=jnp.float32
    ).astype(jnp.bfloat16)
    feed_field = jnp.einsum(
        "aren,aebc->brnc", north_back, east_adjoint, preferred_element_type=jnp.float32
    ).astype(jnp.bfloat16)
    feed_field = feed_field.reshape(2, block_times, local_chans, pol_count, CYL * NSF)
    torque = feed_field[0].astype(jnp.float32) * exchanged[1].astype(jnp.float32) - feed_field[
        1
    ].astype(jnp.float32) * exchanged[0].astype(jnp.float32)
    delay_whole = jnp.einsum(
        "tfpj,f->pj", torque, full_turn * frequency, precision=lax.Precision.HIGHEST
    )
    delay_part = summed_on_arrival(delay_whole.astype(jnp.bfloat16), "feed", 1)
    chan_part = jnp.sum(torque, axis=(0, 3)).T
    band_local = jnp.dot(chan_part, basis, precision=lax.Precision.HIGHEST)
    delay_grad, band_share = in_one((delay_part, band_local), ("chan", "tm"))
    band_grad = taken_together(band_share, "feed")
    return (delay_grad, band_grad)


def solution(mesh):
    in_specs = (
        P(None, "tm", "chan", None, "feed"),
        P(None, "tm", "feed", None, "chan", None, None, None),
        P(),
        P(None, "feed"),
        P(),
        P("tm", "chan"),
        P(),
    )
    out_specs = (P(None, "feed"), P())
    return jax.shard_map(shards, mesh=mesh, in_specs=in_specs, out_specs=out_specs, check_vma=False)
```

profile of v0, /device:TPU:1, one launch (start us, length us, event | category | flops | bytes accessed | tf_op | source)
XLA Modules:
  0.0 166.0 jit_solution(14215627482218629939)
XLA Ops:
  0.7 0.6 copy-done
  1.3 0.2 fusion.77
  1.6 0.8 fusion.75
  2.4 2.6 %fusion.31 = (bf16[1,256,4,2,128]{4,3,2,0,1:T(2,128)(2,1)S(1)}, bf16[1,256,4,2,128]{4,3,2,0,1:T(2,128)(2,1)S(1)}) fusion(f32[4,2,128]{2,1,0:T(2,128)S(1)} %get-tuple-element.17, f32[4,2,128]{2,1,0:T(2,128)S(1)} %get-tuple-element.16, bf16[2,256,4,2,128]{4,3,2,1,0:T(2,128)(2,1)} %param.7), kind=kLoop, calls=%fused_computation.23 | loop fusion | flops 2621440 | bytes 2105344 | tf_op jit(solution)/shard_map/convert.7
  4.9 2.3 %pad_maximum_fusion = bf16[2,256,4,2,128]{4,3,2,0,1:T(2,128)(2,1)} fusion(bf16[1,256,4,2,128]{4,3,2,0,1:T(2,128)(2,1)S(1)} %get-tuple-element.3, bf16[1,256,4,2,128]{4,3,2,0,1:T(2,128)(2,1)S(1)} %get-tuple-element.2), kind=kLoop, calls=%fused_computation.32 | loop fusion | flops 524288 | bytes 2097152 | tf_op jit(solution)/shard_map/stack | solution.py:102
  7.3 13.8 %all-to-all-start = ((bf16[2,256,4,2,128]{4,3,2,0,1:T(2,128)(2,1)}), bf16[2,256,4,2,128]{4,3,2,0,1:T(2,128)(2,1)S(1)}, u32[]{:S(2)}, u32[]{:S(2)}) async-start(bf16[2,256,4,2,128]{4,3,2,0,1:T(2,128)(2,1)} %pad_maximum_fusion), calls=%async_computation | async-start | bytes 2097152 | tf_op jit(solution)/shard_map/all_to_all | solution.py:108
  21.3 0.1 copy.66
  21.5 0.1 mul.391
  21.8 2.2 %fusion.55 = bf16[256,1,512]{2,0,1:T(8,128)(2,1)S(1)} fusion(s32[256]{0:T(256)S(1)} %copy-done.8), kind=kLoop, calls=%fused_computation.69 | loop fusion | flops 2621440 | bytes 263168 | tf_op jit(solution)/shard_map/neg | solution.py:66
  24.0 2.5 %multiply_convert_fusion = (bf16[256,1,512]{2,0,1:T(8,128)(2,1)S(1)}, bf16[256,1,512]{2,0,1:T(8,128)(2,1)S(1)}) fusion(s32[256]{0:T(256)S(1)} %copy-done.8), kind=kLoop, calls=%fused_computation.56 | loop fusion | flops 2490368 | bytes 525312 | tf_op jit(solution)/shard_map/convert_element_type | solution.py:61
  26.5 1.1 maximum_bitcast_fusion.7
  27.5 2.0 %fusion.54 = bf16[512,1,256]{2,0,1:T(8,128)(2,1)S(1)} fusion(s32[256]{0:T(256)S(1)} %copy-done.8), kind=kLoop, calls=%fused_computation.68 | loop fusion | flops 2621440 | bytes 263168 | tf_op jit(solution)/shard_map/neg | solution.py:72
  29.5 2.2 %multiply_convert_fusion.2 = (bf16[512,1,256]{2,0,1:T(8,128)(2,1)S(1)}, bf16[512,1,256]{2,0,1:T(8,128)(2,1)S(1)}) fusion(s32[256]{0:T(256)S(1)} %copy-done.8), kind=kLoop, calls=%fused_computation.60 | loop fusion | flops 2490368 | bytes 525312 | tf_op jit(solution)/shard_map/convert_element_type | solution.py:61
  31.8 1.1 maximum_bitcast_fusion.5
  32.9 2.3 %broadcast_multiply_fusion = f32[64,32,512]{2,1,0:T(8,128)} fusion(f32[32,512]{1,0:T(8,128)S(1)} %copy-done.7, f32[64]{0:T(128)S(1)} %mul.391), kind=kLoop, calls=%fused_computation.15 | loop fusion | flops 1048576 | bytes 4260096 | tf_op jit(solution)/shard_map/mul | solution.py:126
  35.2 10.8 %all-to-all-done = bf16[2,256,4,2,128]{4,3,2,0,1:T(2,128)(2,1)S(1)} async-done(((bf16[2,256,4,2,128]{4,3,2,0,1:T(2,128)(2,1)}), bf16[2,256,4,2,128]{4,3,2,0,1:T(2,128)(2,1)S(1)}, u32[]{:S(2)}, u32[]{:S(2)}) %all-to-all-start) | async-done | bytes 1048608 | tf_op jit(solution)/shard_map/all_to_all | solution.py:108
  46.0 1.2 copy.130
  47.2 7.3 %reshape.563 = bf16[2,64,256,16]{3,2,1,0:T(8,128)(2,1)} reshape(bf16[2,8,4,2,32,128]{5,4,3,2,1,0:T(8,128)(2,1)S(1)} %bitcast.143) | data formatting | bytes 2097152 | tf_op jit(solution)/shard_map/reshape | solution.py:117
  54.5 0.3 slice_convert_fusion.2
  54.8 1.6 reshape.590
  56.5 4.5 %reshape.574 = f32[1,64,256,16]{3,2,1,0:T(8,128)} reshape(f32[1,8,4,2,32,128]{5,4,3,2,1,0:T(8,128)S(1)} %get-tuple-element.6) | data formatting | bytes 2097152 | tf_op jit(solution)/shard_map/convert_element_type | solution.py:135
  60.9 1.5 reshape.591
  62.5 4.5 %reshape.575 = f32[1,64,256,16]{3,2,1,0:T(8,128)} reshape(f32[1,8,4,2,32,128]{5,4,3,2,1,0:T(8,128)S(1)} %get-tuple-element.7) | data formatting | bytes 2097152 | tf_op jit(solution)/shard_map/convert_element_type | solution.py:137
  67.0 6.2 %fusion.18 = bf16[2,64,32,256]{3,2,1,0:T(8,128)(2,1)S(1)} fusion(bf16[2,64,256,16]{3,2,1,0:T(8,128)(2,1)} %reshape.563, bf16[1,16,2,32]{3,1,0,2:T(8,128)(2,1)S(1)} %get-tuple-element.15, bf16[1,16,2,32]{3,1,0,2:T(8,128)(2,1)S(1)} %get-tuple-element.14), kind=kOutput, calls=%fused_computation.16 | convolution fusion | flops 68165632 | bytes 3149824 | tf_op jit(solution)/shard_map/arnc,acbe->bren/dot_general | solution.py:118
  73.2 4.5 %fusion.4 = bf16[2,64,32,512,1]{3,2,1,0,4:T(8,128)(2,1)} fusion(bf16[2,64,32,512]{3,2,1,0:T(8,128)(2,1)S(1)} %bitcast.147, f32[64,32,512]{2,1,0:T(8,128)S(1)} %copy-done.2, bf16[2,64,32,256]{3,2,1,0:T(8,128)(2,1)S(1)} %fusion.18, bf16[1,256,2,512]{3,1,0,2:T(8,128)(2,1)S(1)} %copy-done.4, bf16[1,256,2,512]{3,1,0,2:T(8,128)(2,1)S(1)} %copy-done.3), kind=kOutput, calls=%fused_computation.5 | convolution fusion | flops 2157969408 | bytes 15728640 | tf_op jit(solution)/shard_map/aren,anbm->brem/dot_general | solution.py:121
  77.7 4.8 %fusion.25 = bf16[2,64,256,16]{2,3,1,0:T(8,128)(2,1)S(1)} fusion(bf16[2,64,32,512,1]{3,2,1,0,4:T(8,128)(2,1)} %fusion.4, bf16[1,512,2,256]{3,1,0,2:T(8,128)(2,1)S(1)} %copy-done.6, bf16[1,512,2,256]{3,1,0,2:T(8,128)(2,1)S(1)} %copy-done.5, bf16[1,32,2,16]{1,3,0,2:T(8,128)(2,1)S(1)} %get-tuple-element.13, bf16[1,32,2,16]{1,3,0,2:T(8,128)(2,1)S(1)} %get-tuple-element.12), kind=kOutput, calls=%fused_computation.17 | convolution fusion | flops 2218270720 | bytes 6295552 | tf_op jit(solution)/shard_map/aren,aebc->brnc/dot_general | solution.py:131
  82.6 0.3 slice_convert_fusion.3
  82.8 4.6 %copy.76 = f32[1,64,256,16]{3,2,1,0:T(8,128)} copy(f32[1,64,256,16]{2,3,1,0:T(8,128)S(1)} %get-tuple-element.4) | data formatting | bytes 2097152 | tf_op jit(solution)/shard_map/convert_element_type | solution.py:135
  87.4 6.9 %reshape.570 = f32[8,4,2,4096]{3,2,1,0:T(2,128)S(1)} reshape(f32[1,64,256,16]{3,2,1,0:T(8,128)} %copy.76) | data formatting | bytes 2097152 | tf_op jit(solution)/shard_map/convert_element_type | solution.py:135
  94.3 4.6 %copy.79 = f32[1,64,256,16]{3,2,1,0:T(8,128)} copy(f32[1,64,256,16]{2,3,1,0:T(8,128)S(1)} %get-tuple-element.5) | data formatting | bytes 2097152 | tf_op jit(solution)/shard_map/convert_element_type | solution.py:137
  98.9 7.1 %reshape.572 = f32[8,4,2,4096]{3,2,1,0:T(2,128)S(1)} reshape(f32[1,64,256,16]{3,2,1,0:T(8,128)} %copy.79) | data formatting | bytes 2097152 | tf_op jit(solution)/shard_map/convert_element_type | solution.py:137
  106.0 3.8 %subtract_reduce_fusion.1 = f32[4,2,4096]{2,1,0:T(2,128)S(1)} fusion(f32[8,4,2,4096]{3,2,1,0:T(2,128)S(1)} %reshape.572, f32[8,4,2,4096]{3,2,1,0:T(2,128)} %reshape.591, f32[8,4,2,4096]{3,2,1,0:T(2,128)S(1)} %reshape.570, f32[8,4,2,4096]{3,2,1,0:T(2,128)} %reshape.590), kind=kLoop, calls=%fused_computation.35 | loop fusion | flops 1015808 | bytes 4325376 | tf_op jit(solution)/shard_map/tfpj,f->pj/reduce_sum | solution.py:138
  109.8 0.4 fusion.52
  110.2 0.6 copy.131
  110.8 8.3 %all-to-all-start.1 = ((bf16[32,2,128]{2,1,0:T(2,128)(2,1)}), bf16[32,2,128]{2,1,0:T(2,128)(2,1)S(1)}, u32[]{:S(2)}, u32[]{:S(2)}) async-start(bf16[32,2,128]{2,1,0:T(2,128)(2,1)} %bitcast.142), calls=%async_computation.1 | async-start | bytes 32768 | tf_op jit(solution)/shard_map/all_to_all | solution.py:25
  119.2 5.1 %copy.82 = f32[1,64,256,16]{2,3,1,0:T(8,128)S(1)} copy(f32[1,64,256,16]{3,2,1,0:T(8,128)} %reshape.574) | data formatting | bytes 2097152 | tf_op jit(solution)/shard_map/convert_element_type | solution.py:135
  124.3 5.1 %copy.83 = f32[1,64,256,16]{2,3,1,0:T(8,128)S(1)} copy(f32[1,64,256,16]{3,2,1,0:T(8,128)} %reshape.575) | data formatting | bytes 2097152 | tf_op jit(solution)/shard_map/convert_element_type | solution.py:137
  129.4 0.6 subtract_reduce_fusion
  130.0 0.1 reduce_sum.55
  130.2 0.2 fusion.76
  130.4 0.1 reshape.566
  130.6 15.7 %all_to_all.31 = f32[16,1,288]{2,1,0:T(1,128)S(1)} all-to-all(f32[16,1,288]{2,1,0:T(1,128)S(1)} %broadcast_in_dim.7), channel_id=1, replica_groups=mesh['feed'=32,'chan'=8,'tm'=2] {'chan','tm'}, dimensions={0} | all-to-all | bytes 36864 | tf_op jit(solution)/shard_map/all_to_all | solution.py:31
  146.4 0.1 reshape.568
  146.4 0.6 broadcast_in_dim.8
  147.1 9.5 %all-to-all-start.3 = ((f32[32,2,16]{2,1,0:T(2,128)}), f32[32,2,16]{2,1,0:T(2,128)S(1)}, u32[]{:S(2)}, u32[]{:S(2)}) async-start(f32[32,2,16]{2,1,0:T(2,128)} %broadcast_in_dim.8), calls=%async_computation.3 | async-start | bytes 65536 | tf_op jit(solution)/shard_map/all_to_all | solution.py:31
  156.6 0.6 slice_bitcast_fusion
  157.1 8.2 %all-to-all-done.3 = f32[32,2,16]{2,1,0:T(2,128)S(1)} async-done(((f32[32,2,16]{2,1,0:T(2,128)}), f32[32,2,16]{2,1,0:T(2,128)S(1)}, u32[]{:S(2)}, u32[]{:S(2)}) %all-to-all-start.3) | async-done | bytes 4128 | tf_op jit(solution)/shard_map/all_to_all | solution.py:31
  165.4 0.6 reduce_sum.58
  (38 shorter events, 0.6 us)
Async XLA Ops:
  0.6 0.7 copy-start
  0.6 20.6 %copy-start.9 = (s32[256,4]{0,1:T(4,128)S(1)}, s32[256,4]{0,1:T(4,128)}, u32[]{:S(2)}) copy-start(s32[256,4]{0,1:T(4,128)} %param.12) | copy-start | bytes 12292
  0.7 21.1 %copy-start.8 = (s32[256]{0:T(256)S(1)}, s32[256]{0:T(256)}, u32[]{:S(2)}) copy-start(s32[256]{0:T(256)} %param.13) | copy-start | bytes 3076
  7.3 25.6 %copy-start.7 = (f32[32,512]{1,0:T(8,128)S(1)}, f32[32,512]{1,0:T(8,128)}, u32[]{:S(2)}) copy-start(f32[32,512]{1,0:T(8,128)} %param.9) | copy-start | bytes 196612
  7.3 38.7 %all-to-all-start = ((bf16[2,256,4,2,128]{4,3,2,0,1:T(2,128)(2,1)}), bf16[2,256,4,2,128]{4,3,2,0,1:T(2,128)(2,1)S(1)}, u32[]{:S(2)}, u32[]{:S(2)}) async-start(bf16[2,256,4,2,128]{4,3,2,0,1:T(2,128)(2,1)} %pad_maximum_fusion), calls=%async_computation | async-start | bytes 2097152 | tf_op jit(solution)/shard_map/all_to_all | solution.py:108
  66.9 6.2 %copy-start.2 = (f32[64,32,512]{2,1,0:T(8,128)S(1)}, f32[64,32,512]{2,1,0:T(8,128)}, u32[]{:S(2)}) copy-start(f32[64,32,512]{2,1,0:T(8,128)} %broadcast_multiply_fusion) | copy-start | bytes 12582916
  66.9 6.2 %copy-start.3 = (bf16[1,256,2,512]{3,1,0,2:T(8,128)(2,1)S(1)}, bf16[1,256,2,512]{3,1,0,2:T(8,128)(2,1)}, u32[]{:S(2)}) copy-start(bf16[1,256,2,512]{3,1,0,2:T(8,128)(2,1)} %get-tuple-element.10) | copy-start | bytes 1572868
  66.9 6.2 %copy-start.4 = (bf16[1,256,2,512]{3,1,0,2:T(8,128)(2,1)S(1)}, bf16[1,256,2,512]{3,1,0,2:T(8,128)(2,1)}, u32[]{:S(2)}) copy-start(bf16[1,256,2,512]{3,1,0,2:T(8,128)(2,1)} %get-tuple-element.11) | copy-start | bytes 1572868
  66.9 6.2 %copy-start.10 = (bf16[2,1,1,8,4,2,32,512]{7,6,5,4,3,2,1,0:T(8,128)(2,1)S(1)}, bf16[2,1,1,8,4,2,32,512]{7,6,5,4,3,2,1,0:T(8,128)(2,1)}, u32[]{:S(2)}) copy-start(bf16[2,1,1,8,4,2,32,512]{7,6,5,4,3,2,1,0:T(8,128)(2,1)} %param.8) | copy-start | bytes 12582916
  73.2 4.5 %copy-start.5 = (bf16[1,512,2,256]{3,1,0,2:T(8,128)(2,1)S(1)}, bf16[1,512,2,256]{3,1,0,2:T(8,128)(2,1)}, u32[]{:S(2)}) copy-start(bf16[1,512,2,256]{3,1,0,2:T(8,128)(2,1)} %get-tuple-element.8) | copy-start | bytes 1572868
  73.2 4.5 %copy-start.6 = (bf16[1,512,2,256]{3,1,0,2:T(8,128)(2,1)S(1)}, bf16[1,512,2,256]{3,1,0,2:T(8,128)(2,1)}, u32[]{:S(2)}) copy-start(bf16[1,512,2,256]{3,1,0,2:T(8,128)(2,1)} %get-tuple-element.9) | copy-start | bytes 1572868
  110.8 19.6 %all-to-all-start.1 = ((bf16[32,2,128]{2,1,0:T(2,128)(2,1)}), bf16[32,2,128]{2,1,0:T(2,128)(2,1)S(1)}, u32[]{:S(2)}, u32[]{:S(2)}) async-start(bf16[32,2,128]{2,1,0:T(2,128)(2,1)} %bitcast.142), calls=%async_computation.1 | async-start | bytes 32768 | tf_op jit(solution)/shard_map/all_to_all | solution.py:25
  119.2 46.8 %copy-start.1 = (f32[2,16]{1,0:T(2,128)S(1)}, f32[2,16]{1,0:T(2,128)}, u32[]{:S(2)}) copy-start(f32[2,16]{1,0:T(2,128)} %param.11) | copy-start | bytes 388
  147.1 18.3 %all-to-all-start.3 = ((f32[32,2,16]{2,1,0:T(2,128)}), f32[32,2,16]{2,1,0:T(2,128)S(1)}, u32[]{:S(2)}, u32[]{:S(2)}) async-start(f32[32,2,16]{2,1,0:T(2,128)} %broadcast_in_dim.8), calls=%async_computation.3 | async-start | bytes 65536 | tf_op jit(solution)/shard_map/all_to_all | solution.py:31
where the time goes:
time: 167 us; the launch traced here: 166 us
  local copies, waits for them, and re-layouts  57.1 us (34%)
  starting transfers between devices  31.7 us (19%)
  other arithmetic  25.1 us (15%)
  waiting for transfers between devices  19 us (11%)
  matrix products  16.4 us (10%)
  blocking collectives  15.7 us (9%)
    all_to_all x1, blocking collectives, copy_for_each(): return lax.all_to_all(copies, axis, split_axis=0, concat_axis=0, tiled=True)  15.7 us
    all_to_all x1, starting transfers between devices, shards(): lax.all_to_all(gained, 'feed', split_axis=1, concat_axis=4, tiled=True)  13.8 us
    convert_element_type x2, local copies, waits for them, and re-layouts, shards(): torque = feed_field[0].astype(jnp.float32) * exchanged[1].astype(jnp.floa...  11.7 us
    convert_element_type x2, local copies, waits for them, and re-layouts, shards(): feed_field[0].astype(jnp.float32) * exchanged[1].astype(jnp.float32)  11.4 us
    convert_element_type x3, local copies, waits for them, and re-layouts, shards(): exchanged[1].astype(jnp.float32)  11.2 us
    convert_element_type x3, local copies, waits for them, and re-layouts, shards(): exchanged[0].astype(jnp.float32)  11.1 us
    all_to_all x1, waiting for transfers between devices, shards(): lax.all_to_all(gained, 'feed', split_axis=1, concat_axis=4, tiled=True)  10.8 us
    all_to_all x1, starting transfers between devices, copy_for_each(): return lax.all_to_all(copies, axis, split_axis=0, concat_axis=0, tiled=True)  9.51 us
  transfers between devices with their start and end apart: 3, of which 2 were waited for; matrix products, arithmetic and copies ran while one was open for 16% of the time, Pallas kernels for 0%

commit v1 on v0

v1 whole, which is shorter than its diff:
```python
import math

import jax
import jax.numpy as jnp
import numpy as np
from jax import lax
from jax.experimental import pallas as pl
from jax.experimental.pallas import tpu as pltpu
from jax.sharding import PartitionSpec as P

CYL = 16
NSF = 256
EWB = 32
NSB = 512
BANDS = 16
CHANS = 32
TIMES = 512
FEED = 32
CHUNKS = 4
MESH = pl.DeviceIdType.MESH
full_turn = 2.0 * math.pi
bf16 = jnp.bfloat16
f32 = jnp.float32


def constant_tables():
    e = np.arange(EWB)
    c = np.arange(CYL)
    angle = (np.float32(full_turn / EWB) * ((e[:, None] * c[None, :]) % EWB).astype(np.float32)).astype(np.float32)
    east_real = (np.cos(angle) / np.float32(math.sqrt(EWB))).astype(np.float32)
    east_imag = (-np.sin(angle) / np.float32(math.sqrt(EWB))).astype(np.float32)
    eye = np.eye(8, dtype=np.float32)
    parts = [[east_real, -east_imag], [east_imag, east_real]]
    east = np.zeros((2, 8, EWB, 2, CYL, 8), np.float32)
    for o in range(2):
        for i in range(2):
            east[o, :, :, i] = np.einsum("ec,rs->recs", parts[o][i], eye)
    east = east.reshape(2 * 8 * EWB, 2 * CYL * 8)
    m = np.arange(NSB)
    g = np.arange(NSF)
    angle = (np.float32(full_turn / NSB) * ((m[:, None] * g[None, :]) % NSB).astype(np.float32)).astype(np.float32)
    north_real = (np.cos(angle) / np.float32(math.sqrt(NSB))).astype(np.float32)
    north_imag = (-np.sin(angle) / np.float32(math.sqrt(NSB))).astype(np.float32)
    north_rows = np.concatenate([north_real.T, north_imag.T], 1)
    north_cols = np.concatenate([north_real, north_imag], 0)
    return tuple(jnp.asarray(a, bf16) for a in (east, east.T, north_rows, north_cols))


def iota(shape, dim):
    return lax.broadcasted_iota(jnp.int32, shape, dim)


def dot(a, b):
    return jnp.dot(a, b, preferred_element_type=f32)


def kernel(
    volt_hbm, refs_hbm, weight_hbm, delays_hbm, band_hbm, flags_hbm, grid_hbm,
    east_hbm, east_adj_hbm, rows_hbm, cols_hbm,
    delay_out, band_out,
    volt, refs, weight_ref, delays_ref, band_ref, flags, grid_ref, east_t, east_adj, rows_t, cols_t,
    sky, recv, north, north_adj, keep, flip, vis, gfield, acc, stack,
    piece, piece_in, total, total_in,
    load_sem, recv_sem, send_sem, sum_sem,
):
    feed = lax.axis_index("feed")
    chan = lax.axis_index("chan")
    tm = lax.axis_index("tm")
    ct = chan * 2 + tm
    fx = feed // 8
    fz = feed % 8

    def feed_peer(k):
        return ((fx + k % 4) % 4) * 8 + (fz + k // 4) % 8

    def ct_peer(k):
        return (ct + k) % 16

    barrier = pltpu.get_barrier_semaphore()

    def greet_feed(k, _):
        pl.semaphore_signal(barrier, inc=1, device_id={"feed": feed_peer(k)}, device_id_type=MESH)
        return 0

    def greet_ct(k, _):
        d = ct_peer(k)
        pl.semaphore_signal(barrier, inc=1, device_id={"chan": d // 2, "tm": d % 2}, device_id_type=MESH)
        return 0

    lax.fori_loop(1, FEED, greet_feed, 0)
    lax.fori_loop(1, 16, greet_ct, 0)

    pairs = [
        (delays_hbm, delays_ref), (band_hbm, band_ref), (volt_hbm, volt), (grid_hbm, grid_ref), (flags_hbm, flags),
        (rows_hbm, rows_t), (cols_hbm, cols_t), (weight_hbm, weight_ref), (east_hbm, east_t),
        (east_adj_hbm, east_adj), (refs_hbm, refs),
    ]
    loads = [pltpu.make_async_copy(src, dst, load_sem.at[i]) for i, (src, dst) in enumerate(pairs)]
    for copy in loads:
        copy.start()
    loads[0].wait()
    loads[1].wait()

    row = iota((8, 128), 0)
    lane = iota((8, 128), 1)
    chan_index = (chan * 4 + row // 2).astype(f32)
    freq_turn = full_turn * (0.4 + 0.4 * (chan_index + 0.5) / CHANS)
    first_pol = row % 2 == 0

    def basis_at(term):
        return math.sqrt(2.0 / CHANS) * jnp.cos(math.pi * (chan_index + 0.5) * term.astype(f32) / CHANS)

    basis = basis_at(lane % BANDS)
    coef = jnp.where(first_pol[:, :BANDS], band_ref[0:1, :], band_ref[1:2, :])
    offset = jnp.sum(coef * basis[:, :BANDS], axis=1, keepdims=True)
    phases = freq_turn * jnp.where(first_pol, delays_ref[0:1, :], delays_ref[1:2, :]) + offset
    gain_real = jnp.cos(phases)
    gain_imag = -jnp.sin(phases)
    gain_real = jnp.concatenate([gain_real, gain_real], 0)
    gain_imag = jnp.concatenate([gain_imag, gain_imag], 0)
    loads[2].wait()

    def gain_block(d, _):
        for q in range(CHUNKS):
            volt_real = volt[0, d, q].astype(f32)
            volt_imag = volt[1, d, q].astype(f32)
            sky[q, d, 0:16, :] = (gain_real * volt_real - gain_imag * volt_imag).astype(bf16)
            sky[q, d, 16:32, :] = (gain_real * volt_imag + gain_imag * volt_real).astype(bf16)
        return 0

    lax.fori_loop(0, FEED, gain_block, 0)
    pl.semaphore_wait(barrier, FEED - 1 + 15)

    def send_chunk(q, _):
        pltpu.make_async_copy(sky.at[q, feed], recv.at[q, feed], recv_sem.at[q]).start()

        def send(k, _):
            d = feed_peer(k)
            pltpu.make_async_remote_copy(
                src_ref=sky.at[q, d],
                dst_ref=recv.at[q, feed],
                send_sem=send_sem.at[q],
                recv_sem=recv_sem.at[q],
                device_id={"feed": d},
                device_id_type=MESH,
            ).start()
            return 0

        lax.fori_loop(1, FEED, send, 0)
        return 0

    lax.fori_loop(0, CHUNKS, send_chunk, 0)

    for copy in loads[3:]:
        copy.wait()
    pick_t = jnp.where(iota((NSF, NSF), 0) == grid_ref[...], 1.0, 0.0).astype(f32)
    pick = jnp.transpose(pick_t).astype(bf16)
    pick_t = pick_t.astype(bf16)
    by_n = dot(pick, rows_t[...]).astype(bf16)
    north[0:NSF, :] = by_n
    north[NSF:, 0:NSB] = -by_n[:, NSB:]
    north[NSF:, NSB:] = by_n[:, :NSB]
    by_m = dot(cols_t[...], pick_t).astype(bf16)
    north_adj[0:NSB, 0:NSF] = by_m[:NSB]
    north_adj[0:NSB, NSF:] = -by_m[NSB:]
    north_adj[NSB:, 0:NSF] = by_m[NSB:]
    north_adj[NSB:, NSF:] = by_m[:NSB]
    kept = (1 - flags[...]).astype(f32) * (1.0 / TIMES)
    kept = jnp.concatenate([kept[i // 2 : i // 2 + 1] for i in range(8)], 0)
    for t in range(8):
        at_time = jnp.where(iota((8, NSF), 1) == feed * 8 + t, kept, 0.0)
        keep[t] = jnp.broadcast_to(jnp.sum(at_time, axis=1, keepdims=True), (8, NSF))
    acc[...] = jnp.zeros_like(acc)
    stack[...] = jnp.zeros_like(stack)
    low = iota((32, 128), 1) < 64

    def chunk(q, _):
        pltpu.make_async_copy(recv.at[q], recv.at[q], recv_sem.at[q]).wait()
        for g in range(8):
            block = jnp.concatenate([recv[q, g + 8 * s] for s in range(4)], 0)
            flip[g * 128 : (g + 1) * 128, :] = jnp.transpose(block.astype(f32))
        for h in range(8):
            pair = jnp.concatenate(
                [flip[pl.ds(2 * h, 64, stride=16), :], flip[pl.ds(2 * h + 1, 64, stride=16), :]], 0
            )
            back = jnp.transpose(pair)
            u = [back[32 * s : 32 * (s + 1)] for s in range(4)]
            v = [pltpu.roll(a, 64, 1) for a in u]
            halves = [
                [jnp.where(low, u[0], v[1]), jnp.where(low, u[2], v[3])],
                [jnp.where(low, v[0], u[1]), jnp.where(low, v[2], u[3])],
            ]
            for i in range(2):
                at = (2 * h + i) * 16
                for b in range(2):
                    both = halves[i][b].astype(bf16)
                    vis[at : at + 16, b * 128 : (b + 1) * 128] = both[0:16]
                    vis[at : at + 16, NSF + b * 128 : NSF + (b + 1) * 128] = both[16:32]
        north_out = dot(vis[...], north[...]).reshape(CYL, 16, 2 * NSB)
        for t in range(2):
            one = north_out[:, 8 * t : 8 * t + 8, :].reshape(CYL * 8, 2 * NSB)
            one = jnp.concatenate([one[:, :NSB], one[:, NSB:]], 0).astype(bf16)
            beams = dot(east_t[...], one)
            first = pl.multiple_of(q * 16 + t * 8, 8)
            seen = refs[:, pl.ds(first, 8)].reshape(2 * 8 * EWB, NSB).astype(f32)
            resid = ((beams - seen).reshape(16, EWB, NSB) * weight_ref[...][None]).reshape(2 * 8 * EWB, NSB)
            adj = dot(east_adj[...], resid.astype(bf16)).astype(bf16)
            gfield[128 * t : 128 * (t + 1), 0:NSB] = adj[0:128]
            gfield[128 * t : 128 * (t + 1), NSB:] = adj[128:256]
        field = dot(gfield[...], north_adj[...])
        here = vis[...].astype(f32).reshape(CYL, 16, 2 * NSF)
        for t in range(2):
            f = field[128 * t : 128 * (t + 1)].reshape(CYL, 8, 2 * NSF)
            s = here[:, 8 * t : 8 * t + 8, :]
            torque = f[:, :, :NSF] * s[:, :, NSF:] - f[:, :, NSF:] * s[:, :, :NSF]
            acc[...] += torque * keep[2 * q + t][None]
        return 0

    lax.fori_loop(0, CHUNKS, chunk, 0)

    def over_chans(x):
        x = x + pltpu.roll(x, 4, 0)
        return x + pltpu.roll(x, 2, 0)

    wide_turn = jnp.concatenate([freq_turn, freq_turn], 1)
    for c in range(CYL):
        summed = over_chans(acc[c] * wide_turn)
        stack[c : c + 1, :] = summed[0:1]
        stack[CYL + c : CYL + c + 1, :] = summed[1:2]
    chan_sum = jnp.sum(jnp.sum(acc[...], axis=0), axis=1, keepdims=True)
    band_lanes = (lane >= 32) & (lane < 32 + BANDS)
    band = over_chans(jnp.where(band_lanes, basis * chan_sum, 0.0))
    band_high = band.astype(bf16).astype(f32)
    band = jnp.where(row < 2, band_high, jnp.where(row < 4, band - band_high, 0.0))
    for h in range(2):
        part = jnp.transpose(stack[:, 128 * h : 128 * (h + 1)]).reshape(16, 8, 128)
        piece[16 * h : 16 * (h + 1)] = (part + band[None]).astype(bf16)

    pltpu.make_async_copy(piece.at[feed], piece_in.at[feed], sum_sem.at[0]).start()

    def send_piece(k, _):
        d = feed_peer(k)
        pltpu.make_async_remote_copy(
            src_ref=piece.at[d],
            dst_ref=piece_in.at[feed],
            send_sem=sum_sem.at[1],
            recv_sem=sum_sem.at[0],
            device_id={"feed": d},
            device_id_type=MESH,
        ).start()
        return 0

    lax.fori_loop(1, FEED, send_piece, 0)
    pltpu.make_async_copy(piece_in, piece_in, sum_sem.at[0]).wait()
    total[...] = jnp.sum(piece_in[...].astype(f32), axis=0)

    pltpu.make_async_copy(total, total_in.at[ct], sum_sem.at[2]).start()

    def send_total(k, _):
        d = ct_peer(k)
        pltpu.make_async_remote_copy(
            src_ref=total,
            dst_ref=total_in.at[ct],
            send_sem=sum_sem.at[3],
            recv_sem=sum_sem.at[2],
            device_id={"chan": d // 2, "tm": d % 2},
            device_id_type=MESH,
        ).start()
        return 0

    lax.fori_loop(1, 16, send_total, 0)
    for q in range(CHUNKS):
        pltpu.make_async_copy(sky.at[q, pl.ds(0, FEED - 1)], sky.at[q, pl.ds(0, FEED - 1)], send_sem.at[q]).wait()
    some = piece.at[pl.ds(0, FEED - 1)]
    pltpu.make_async_copy(some, some, sum_sem.at[1]).wait()
    pltpu.make_async_copy(total_in, total_in, sum_sem.at[2]).wait()
    grad = jnp.sum(total_in[...], axis=0)
    own = (lane // 16) == row
    for p in range(2):
        shifted = pltpu.roll(grad, 112, 1) if p else grad
        turned = pltpu.roll(shifted, 0, 1, stride=16, stride_axis=0)
        delay_out[p : p + 1, :] = jnp.sum(jnp.where(own, turned, 0.0), axis=0, keepdims=True)
    band = pltpu.roll(grad + pltpu.roll(grad, 6, 0), 96, 1)
    band_out[...] = band[0:2, 0:BANDS]
    some = total_in.at[pl.ds(0, 15)]
    pltpu.make_async_copy(some, some, sum_sem.at[3]).wait()


def shards(voltages, beam_refs, beam_weight, delays, band_phase, rfi_flags, grid_rows):
    hbm_spec = pl.BlockSpec(memory_space=pltpu.MemorySpace.HBM)
    vmem_spec = pl.BlockSpec(memory_space=pltpu.VMEM)
    east, east_adj, rows, cols = constant_tables()
    return pl.pallas_call(
        kernel,
        out_shape=(jax.ShapeDtypeStruct((2, 128), f32), jax.ShapeDtypeStruct((2, BANDS), f32)),
        in_specs=[hbm_spec] * 11,
        out_specs=(vmem_spec, vmem_spec),
        scratch_shapes=[
            pltpu.VMEM((2, FEED, CHUNKS, 16, 128), bf16),
            pltpu.VMEM((2, 64, EWB, NSB), bf16),
            pltpu.VMEM((EWB, NSB), f32),
            pltpu.VMEM((2, 128), f32),
            pltpu.VMEM((2, BANDS), f32),
            pltpu.VMEM((4, NSF), jnp.int32),
            pltpu.VMEM((1, NSF), jnp.int32),
            pltpu.VMEM((512, 256), bf16),
            pltpu.VMEM((256, 512), bf16),
            pltpu.VMEM((256, 1024), bf16),
            pltpu.VMEM((1024, 256), bf16),
            pltpu.VMEM((CHUNKS, FEED, 32, 128), bf16),
            pltpu.VMEM((CHUNKS, FEED, 32, 128), bf16),
            pltpu.VMEM((2 * NSF, 2 * NSB), bf16),
            pltpu.VMEM((2 * NSB, 2 * NSF), bf16),
            pltpu.VMEM((8, 8, NSF), f32),
            pltpu.VMEM((8 * 128, 128), f32),
            pltpu.VMEM((256, 2 * NSF), bf16),
            pltpu.VMEM((256, 2 * NSB), bf16),
            pltpu.VMEM((CYL, 8, NSF), f32),
            pltpu.VMEM((128, NSF), f32),
            pltpu.VMEM((FEED, 8, 128), bf16),
            pltpu.VMEM((FEED, 8, 128), bf16),
            pltpu.VMEM((8, 128), f32),
            pltpu.VMEM((16, 8, 128), f32),
            pltpu.SemaphoreType.DMA((11,)),
            pltpu.SemaphoreType.DMA((CHUNKS,)),
            pltpu.SemaphoreType.DMA((CHUNKS,)),
            pltpu.SemaphoreType.DMA((4,)),
        ],
        compiler_params=pltpu.CompilerParams(
            collective_id=0, has_side_effects=True, vmem_limit_bytes=67043328
        ),
    )(
        voltages.reshape(2, FEED, CHUNKS, 16, 128),
        beam_refs.reshape(2, 64, EWB, NSB),
        beam_weight,
        delays,
        band_phase,
        rfi_flags.T,
        grid_rows.reshape(1, NSF),
        east,
        east_adj,
        rows,
        cols,
    )


def solution(mesh):
    in_specs = (
        P(None, "tm", "chan", None, "feed"),
        P(None, "tm", "feed", None, "chan", None, None, None),
        P(),
        P(None, "feed"),
        P(),
        P("tm", "chan"),
        P(),
    )
    out_specs = (P(None, "feed"), P())
    return jax.shard_map(shards, mesh=mesh, in_specs=in_specs, out_specs=out_specs, check_vma=False)
```

time: 167 us -> 61.1 us (0.37)
  Pallas kernels: 0 us -> 57.9 us
  local copies, waits for them, and re-layouts: 57.1 us -> 2.44 us
  starting transfers between devices: 31.7 us -> 0 us
  other arithmetic: 25.1 us -> 0 us
  waiting for transfers between devices: 19 us -> 0 us
  matrix products: 16.4 us -> 0 us
  blocking collectives: 15.7 us -> 0 us
    pallas_call x0 -> x1, Pallas kernels: none -> 57.9 us  [shards(): pl.pallas_call(kernel, out_shape=(jax.ShapeDtypeStruct((2, 128), f32), ja...]
    convert_element_type x10 -> x0, local copies, waits for them, and re-layouts: 45.4 us -> none  [the longest x2 11.7 us: shards(): torque = feed_field[0].astype(jnp.float32) * exchanged[1].astype(jnp.floa...]
    all_to_all x3 -> x0, starting transfers between devices: 31.7 us -> none  [the longest x1 13.8 us: shards(): lax.all_to_all(gained, 'feed', split_axis=1, concat_axis=4, tiled=True)]
    all_to_all x3 -> x0, waiting for transfers between devices: 19 us -> none  [the longest x1 10.8 us: shards(): lax.all_to_all(gained, 'feed', split_axis=1, concat_axis=4, tiled=True)]
    dot_general x6 -> x0, matrix products: 16.4 us -> none  [the longest x1 6.21 us: shards(): jnp.einsum('arnc,acbe->bren', sectioned, east_forward, preferred_element_...]
    all_to_all x1 -> x0, blocking collectives: 15.7 us -> none  [copy_for_each(): return lax.all_to_all(copies, axis, split_axis=0, concat_axis=0, tiled=True)]
    reshape x4 -> x0, local copies, waits for them, and re-layouts: 8.07 us -> none  [the longest x1 7.34 us: shards(): sectioned = exchanged.reshape(2, row_count, NSF, CYL)]
    another operation x6 -> x0, other arithmetic: 7.09 us -> none
  transfers between devices with their start and end apart: 3 -> 0, of which waited for: 2 -> 0; matrix products, arithmetic and copies ran while one was open for 16% -> 0% of each run, Pallas kernels for 0% -> 0%
where the time goes in v1:
time: 61.1 us; the launch traced here: 60.9 us
  Pallas kernels  57.9 us (95%)
  local copies, waits for them, and re-layouts  2.44 us (4%)
  between operations  0.64 us (1%)
    pallas_call x1, Pallas kernels, shards(): pl.pallas_call(kernel, out_shape=(jax.ShapeDtypeStruct((2, 128), f32), ja...  57.9 us
    unnamed x2, local copies, waits for them, and re-layouts  2.44 us

profile of v1, /device:TPU:1, one launch (start us, length us, event | category | flops | bytes accessed | tf_op | source)
XLA Modules:
  0.0 60.9 jit_solution(11076681364190545165)
XLA Ops:
  0.6 57.9 %shard_map.122 = (f32[2,128]{1,0:T(2,128)}, f32[2,16]{1,0:T(2,128)}) custom-call(bf16[2,32,4,16,128]{4,3,2,1,0:T(8,128)(2,1)} %bitcast.5, bf16[2,64,32,512]{3,2,1,0:T(8,128)(2,1)} %bitcast.4, f32[32,512]{1,0:T(8,128)} %weight_hbm.1, f32[2,128]{1,0:T(2,128)} %delays_hbm.1, f32[2,16]{1,0:T(2,128)} %band_hbm.1, s32[4,256]{1,0:T(4,128)} %bitcast.6, ...), custom_call_target="tpu_custom_call" | custom-call | tf_op jit(solution)/shard_map/pallas_call | solution.py:293
  58.5 1.2 %copy.15 = f32[2,128]{1,0:T(2,128)} copy(f32[2,128]{1,0:T(2,128)} %get-tuple-element.4) | data formatting | bytes 2048
  59.7 1.2 %copy.16 = f32[2,16]{1,0:T(2,128)} copy(f32[2,16]{1,0:T(2,128)} %get-tuple-element.5) | data formatting | bytes 256

commit v2 on v1

--- a/solution.py
+++ b/solution.py
@@ -54,10 +54,17 @@
     return jnp.dot(a, b, preferred_element_type=f32)
 
 
+def spread(size):
+    return [(size // 2 + (i + 1) // 2 * (-1) ** i) % size for i in range(size)]
+
+
+OFFSETS = [(dx, dz) for dx in spread(4) for dz in spread(8)][:-1]
+
+
 def kernel(
     volt_hbm, refs_hbm, weight_hbm, delays_hbm, band_hbm, flags_hbm, grid_hbm,
     east_hbm, east_adj_hbm, rows_hbm, cols_hbm,
-    delay_out, band_out,
+    out,
     volt, refs, weight_ref, delays_ref, band_ref, flags, grid_ref, east_t, east_adj, rows_t, cols_t,
     sky, recv, north, north_adj, keep, flip, vis, gfield, acc, stack,
     piece, piece_in, total, total_in,
@@ -70,25 +77,24 @@
     fx = feed // 8
     fz = feed % 8
 
-    def feed_peer(k):
-        return ((fx + k % 4) % 4) * 8 + (fz + k // 4) % 8
+    def feed_peer(offset):
+        return ((fx + offset[0]) % 4) * 8 + (fz + offset[1]) % 8
 
     def ct_peer(k):
-        return (ct + k) % 16
+        dy = 4 + (k // 2 + 1) // 2 * (1 - 2 * (k // 2 % 2))
+        return (chan + dy) % 8, (tm + 1 - k % 2) % 2
 
     barrier = pltpu.get_barrier_semaphore()
 
-    def greet_feed(k, _):
-        pl.semaphore_signal(barrier, inc=1, device_id={"feed": feed_peer(k)}, device_id_type=MESH)
-        return 0
+    for offset in OFFSETS:
+        pl.semaphore_signal(barrier, inc=1, device_id={"feed": feed_peer(offset)}, device_id_type=MESH)
 
     def greet_ct(k, _):
-        d = ct_peer(k)
-        pl.semaphore_signal(barrier, inc=1, device_id={"chan": d // 2, "tm": d % 2}, device_id_type=MESH)
-        return 0
-
-    lax.fori_loop(1, FEED, greet_feed, 0)
-    lax.fori_loop(1, 16, greet_ct, 0)
+        y, core = ct_peer(k)
+        pl.semaphore_signal(barrier, inc=1, device_id={"chan": y, "tm": core}, device_id_type=MESH)
+        return 0
+
+    lax.fori_loop(0, 15, greet_ct, 0)
 
     pairs = [
         (delays_hbm, delays_ref), (band_hbm, band_ref), (volt_hbm, volt), (grid_hbm, grid_ref), (flags_hbm, flags),
@@ -134,8 +140,8 @@
     def send_chunk(q, _):
         pltpu.make_async_copy(sky.at[q, feed], recv.at[q, feed], recv_sem.at[q]).start()
 
-        def send(k, _):
-            d = feed_peer(k)
+        for offset in OFFSETS:
+            d = feed_peer(offset)
             pltpu.make_async_remote_copy(
                 src_ref=sky.at[q, d],
                 dst_ref=recv.at[q, feed],
@@ -144,9 +150,6 @@
                 device_id={"feed": d},
                 device_id_type=MESH,
             ).start()
-            return 0
-
-        lax.fori_loop(1, FEED, send, 0)
         return 0
 
     lax.fori_loop(0, CHUNKS, send_chunk, 0)
@@ -231,15 +234,17 @@
     band_lanes = (lane >= 32) & (lane < 32 + BANDS)
     band = over_chans(jnp.where(band_lanes, basis * chan_sum, 0.0))
     band_high = band.astype(bf16).astype(f32)
-    band = jnp.where(row < 2, band_high, jnp.where(row < 4, band - band_high, 0.0))
+    band = jnp.where(row % 4 < 2, band_high, band - band_high)
     for h in range(2):
-        part = jnp.transpose(stack[:, 128 * h : 128 * (h + 1)]).reshape(16, 8, 128)
-        piece[16 * h : 16 * (h + 1)] = (part + band[None]).astype(bf16)
+        flip[128 * h : 128 * (h + 1), :] = jnp.transpose(stack[:, 128 * h : 128 * (h + 1)])
+    packed = flip[pl.ds(0, 128, stride=2), :] + pltpu.roll(flip[pl.ds(1, 128, stride=2), :], 64, 1)
+    packed = (packed.reshape(16, 8, 128) + band[None]).reshape(FEED, 4, 128)
+    piece[...] = packed.astype(bf16)
 
     pltpu.make_async_copy(piece.at[feed], piece_in.at[feed], sum_sem.at[0]).start()
 
-    def send_piece(k, _):
-        d = feed_peer(k)
+    for offset in OFFSETS:
+        d = feed_peer(offset)
         pltpu.make_async_remote_copy(
             src_ref=piece.at[d],
             dst_ref=piece_in.at[feed],
@@ -248,53 +253,53 @@
             device_id={"feed": d},
             device_id_type=MESH,
         ).start()
-        return 0
-
-    lax.fori_loop(1, FEED, send_piece, 0)
     pltpu.make_async_copy(piece_in, piece_in, sum_sem.at[0]).wait()
     total[...] = jnp.sum(piece_in[...].astype(f32), axis=0)
 
     pltpu.make_async_copy(total, total_in.at[ct], sum_sem.at[2]).start()
 
     def send_total(k, _):
-        d = ct_peer(k)
+        y, core = ct_peer(k)
         pltpu.make_async_remote_copy(
             src_ref=total,
             dst_ref=total_in.at[ct],
             send_sem=sum_sem.at[3],
             recv_sem=sum_sem.at[2],
-            device_id={"chan": d // 2, "tm": d % 2},
+            device_id={"chan": y, "tm": core},
             device_id_type=MESH,
         ).start()
         return 0
 
-    lax.fori_loop(1, 16, send_total, 0)
+    lax.fori_loop(0, 15, send_total, 0)
     for q in range(CHUNKS):
         pltpu.make_async_copy(sky.at[q, pl.ds(0, FEED - 1)], sky.at[q, pl.ds(0, FEED - 1)], send_sem.at[q]).wait()
     some = piece.at[pl.ds(0, FEED - 1)]
     pltpu.make_async_copy(some, some, sum_sem.at[1]).wait()
     pltpu.make_async_copy(total_in, total_in, sum_sem.at[2]).wait()
     grad = jnp.sum(total_in[...], axis=0)
-    own = (lane // 16) == row
+    pair = iota((4, 128), 0)
+    slot = iota((4, 128), 1) // 16
     for p in range(2):
-        shifted = pltpu.roll(grad, 112, 1) if p else grad
-        turned = pltpu.roll(shifted, 0, 1, stride=16, stride_axis=0)
-        delay_out[p : p + 1, :] = jnp.sum(jnp.where(own, turned, 0.0), axis=0, keepdims=True)
-    band = pltpu.roll(grad + pltpu.roll(grad, 6, 0), 96, 1)
-    band_out[...] = band[0:2, 0:BANDS]
+        delay = jnp.zeros((4, 128), f32)
+        for h in range(2):
+            for r in range(4):
+                turned = pltpu.roll(grad, (32 * r - 48 * h - 16 * p) % 128, 1)
+                delay = jnp.where((pair == r) & (slot == 2 * r + h), turned, delay)
+        out[p : p + 1, :] = jnp.sum(delay, axis=0, keepdims=True)
+    band = pltpu.roll(grad, 96, 1)
+    out[2:4, :] = band[0:2] + band[2:4]
     some = total_in.at[pl.ds(0, 15)]
     pltpu.make_async_copy(some, some, sum_sem.at[3]).wait()
 
 
 def shards(voltages, beam_refs, beam_weight, delays, band_phase, rfi_flags, grid_rows):
     hbm_spec = pl.BlockSpec(memory_space=pltpu.MemorySpace.HBM)
-    vmem_spec = pl.BlockSpec(memory_space=pltpu.VMEM)
     east, east_adj, rows, cols = constant_tables()
-    return pl.pallas_call(
+    grads = pl.pallas_call(
         kernel,
-        out_shape=(jax.ShapeDtypeStruct((2, 128), f32), jax.ShapeDtypeStruct((2, BANDS), f32)),
+        out_shape=jax.ShapeDtypeStruct((4, 128), f32),
         in_specs=[hbm_spec] * 11,
-        out_specs=(vmem_spec, vmem_spec),
+        out_specs=pl.BlockSpec(memory_space=pltpu.VMEM),
         scratch_shapes=[
             pltpu.VMEM((2, FEED, CHUNKS, 16, 128), bf16),
             pltpu.VMEM((2, 64, EWB, NSB), bf16),
@@ -317,19 +322,19 @@
             pltpu.VMEM((256, 2 * NSB), bf16),
             pltpu.VMEM((CYL, 8, NSF), f32),
             pltpu.VMEM((128, NSF), f32),
-            pltpu.VMEM((FEED, 8, 128), bf16),
-            pltpu.VMEM((FEED, 8, 128), bf16),
-            pltpu.VMEM((8, 128), f32),
-            pltpu.VMEM((16, 8, 128), f32),
+            pltpu.VMEM((FEED, 4, 128), bf16),
+            pltpu.VMEM((FEED, 4, 128), bf16),
+            pltpu.VMEM((4, 128), f32),
+            pltpu.VMEM((16, 4, 128), f32),
             pltpu.SemaphoreType.DMA((11,)),
             pltpu.SemaphoreType.DMA((CHUNKS,)),
             pltpu.SemaphoreType.DMA((CHUNKS,)),
             pltpu.SemaphoreType.DMA((4,)),
         ],
         compiler_params=pltpu.CompilerParams(
-            collective_id=0, has_side_effects=True, vmem_limit_bytes=67043328
+            collective_id=0, has_side_effects=True, vmem_limit_bytes=56000000
         ),
-    )(
+    )(*[pltpu.with_memory_space_constraint(a, pltpu.MemorySpace.HBM) for a in (
         voltages.reshape(2, FEED, CHUNKS, 16, 128),
         beam_refs.reshape(2, 64, EWB, NSB),
         beam_weight,
@@ -341,7 +346,8 @@
         east_adj,
         rows,
         cols,
-    )
+        )])
+    return grads[0:2], grads[2:4, 0:BANDS]
 
 
 def solution(mesh):

time: 61.1 us -> 56.7 us (0.928)
  Pallas kernels: 57.9 us -> 54.9 us
  local copies, waits for them, and re-layouts: 2.44 us -> 1.13 us
    pallas_call x1, Pallas kernels: 57.9 us -> 54.9 us  [shards(): pl.pallas_call(kernel, out_shape=jax.ShapeDtypeStruct((4, 128), f32), in_...]
    unnamed x2 -> x0, local copies, waits for them, and re-layouts: 2.44 us -> none
    slice x0 -> x2, local copies, waits for them, and re-layouts: none -> 1.13 us  [shards(): return (grads[0:2], grads[2:4, 0:BANDS])]
where the time goes in v2:
time: 56.7 us; the launch traced here: 56.6 us
  Pallas kernels  54.9 us (97%)
  local copies, waits for them, and re-layouts  1.13 us (2%)
  between operations  0.64 us (1%)
    pallas_call x1, Pallas kernels, shards(): pl.pallas_call(kernel, out_shape=jax.ShapeDtypeStruct((4, 128), f32), in_...  54.9 us

profile of v2, /device:TPU:1, one launch (start us, length us, event | category | flops | bytes accessed | tf_op | source)
XLA Modules:
  0.0 56.6 jit_solution(16351927465364163989)
XLA Ops:
  0.6 54.9 %shard_map.122 = f32[4,128]{1,0:T(4,128)S(1)} custom-call(bf16[2,32,4,16,128]{4,3,2,1,0:T(8,128)(2,1)} %bitcast.5, bf16[2,64,32,512]{3,2,1,0:T(8,128)(2,1)} %bitcast.4, f32[32,512]{1,0:T(8,128)} %weight_hbm.1, f32[2,128]{1,0:T(2,128)} %delays_hbm.1, f32[2,16]{1,0:T(2,128)} %band_hbm.1, s32[4,256]{1,0:T(4,128)} %bitcast.6, s32[1,256]{1,0:T(1,128)} %bitcast.7, ...), custom_call_target="tpu_custom_call" | custom-call | tf_op jit(solution)/shard_map/pallas_call | solution.py:298
  55.5 0.6 slice.7
  56.1 0.6 slice.6

commit v3 on v2

--- a/solution.py
+++ b/solution.py
@@ -59,6 +59,7 @@
 
 
 OFFSETS = [(dx, dz) for dx in spread(4) for dz in spread(8)][:-1]
+MESSAGES = ((0, 4), (4, 7), (7, 8))
 
 
 def kernel(
@@ -130,29 +131,28 @@
         for q in range(CHUNKS):
             volt_real = volt[0, d, q].astype(f32)
             volt_imag = volt[1, d, q].astype(f32)
-            sky[q, d, 0:16, :] = (gain_real * volt_real - gain_imag * volt_imag).astype(bf16)
-            sky[q, d, 16:32, :] = (gain_real * volt_imag + gain_imag * volt_real).astype(bf16)
+            sky_real = gain_real * volt_real - gain_imag * volt_imag
+            sky_imag = gain_real * volt_imag + gain_imag * volt_real
+            for t in range(2):
+                sky[d, 2 * q + t, 0] = sky_real[8 * t : 8 * t + 8].astype(bf16)
+                sky[d, 2 * q + t, 1] = sky_imag[8 * t : 8 * t + 8].astype(bf16)
         return 0
 
     lax.fori_loop(0, FEED, gain_block, 0)
     pl.semaphore_wait(barrier, FEED - 1 + 15)
 
-    def send_chunk(q, _):
-        pltpu.make_async_copy(sky.at[q, feed], recv.at[q, feed], recv_sem.at[q]).start()
-
+    for m, (first, last) in enumerate(MESSAGES):
+        pltpu.make_async_copy(sky.at[feed, first:last], recv.at[feed, first:last], recv_sem.at[m]).start()
         for offset in OFFSETS:
             d = feed_peer(offset)
             pltpu.make_async_remote_copy(
-                src_ref=sky.at[q, d],
-                dst_ref=recv.at[q, feed],
-                send_sem=send_sem.at[q],
-                recv_sem=recv_sem.at[q],
+                src_ref=sky.at[d, first:last],
+                dst_ref=recv.at[feed, first:last],
+                send_sem=send_sem.at[m],
+                recv_sem=recv_sem.at[m],
                 device_id={"feed": d},
                 device_id_type=MESH,
             ).start()
-        return 0
-
-    lax.fori_loop(0, CHUNKS, send_chunk, 0)
 
     for copy in loads[3:]:
         copy.wait()
@@ -177,16 +177,26 @@
     stack[...] = jnp.zeros_like(stack)
     low = iota((32, 128), 1) < 64
 
-    def chunk(q, _):
-        pltpu.make_async_copy(recv.at[q], recv.at[q], recv_sem.at[q]).wait()
+    def arrived(time):
+        for m, (first, last) in enumerate(MESSAGES):
+
+            @pl.when(time == first)
+            def _():
+                part = recv.at[:, first:last]
+                pltpu.make_async_copy(part, part, recv_sem.at[m]).wait()
+
+    def place(at, rows, both):
+        for b in range(2):
+            vis[at : at + rows, b * 128 : (b + 1) * 128] = both[b][0:rows].astype(bf16)
+            vis[at : at + rows, NSF + b * 128 : NSF + (b + 1) * 128] = both[b][rows : 2 * rows].astype(bf16)
+
+    def gather_pair(time):
         for g in range(8):
-            block = jnp.concatenate([recv[q, g + 8 * s] for s in range(4)], 0)
-            flip[g * 128 : (g + 1) * 128, :] = jnp.transpose(block.astype(f32))
+            block = [recv[g + 8 * s, pl.ds(time, 2)].astype(f32).reshape(32, 128) for s in range(4)]
+            flip[g * 128 : (g + 1) * 128, :] = jnp.transpose(jnp.concatenate(block, 0))
         for h in range(8):
-            pair = jnp.concatenate(
-                [flip[pl.ds(2 * h, 64, stride=16), :], flip[pl.ds(2 * h + 1, 64, stride=16), :]], 0
-            )
-            back = jnp.transpose(pair)
+            pair = [flip[pl.ds(2 * h + i, 64, stride=16), :] for i in range(2)]
+            back = jnp.transpose(jnp.concatenate(pair, 0))
             u = [back[32 * s : 32 * (s + 1)] for s in range(4)]
             v = [pltpu.roll(a, 64, 1) for a in u]
             halves = [
@@ -194,32 +204,66 @@
                 [jnp.where(low, v[0], u[1]), jnp.where(low, v[2], u[3])],
             ]
             for i in range(2):
-                at = (2 * h + i) * 16
+                both = [jnp.concatenate([a[0:8], a[16:24], a[8:16], a[24:32]], 0) for a in halves[i]]
+                place((2 * h + i) * 16, 16, both)
+
+    quarter = iota((16, 128), 1) // 32
+
+    def gather_one(time):
+        for g in range(4):
+            block = [recv[4 * s + g, time].astype(f32).reshape(16, 128) for s in range(8)]
+            flip[g * 128 : (g + 1) * 128, :] = jnp.transpose(jnp.concatenate(block, 0))
+        for h in range(4):
+            four = [flip[pl.ds(4 * h + i, 32, stride=16), :] for i in range(4)]
+            back = jnp.transpose(jnp.concatenate(four, 0))
+            u = [back[16 * s : 16 * (s + 1)] for s in range(8)]
+            for i in range(4):
+                both = []
                 for b in range(2):
-                    both = halves[i][b].astype(bf16)
-                    vis[at : at + 16, b * 128 : (b + 1) * 128] = both[0:16]
-                    vis[at : at + 16, NSF + b * 128 : NSF + (b + 1) * 128] = both[16:32]
-        north_out = dot(vis[...], north[...]).reshape(CYL, 16, 2 * NSB)
-        for t in range(2):
+                    half = jnp.zeros((16, 128), f32)
+                    for j in range(4):
+                        shift = 32 * (j - i) % 128
+                        moved = pltpu.roll(u[4 * b + j], shift, 1) if shift else u[4 * b + j]
+                        half = jnp.where(quarter == j, moved, half)
+                    both.append(half)
+                place((4 * h + i) * 8, 8, both)
+
+    def gradient(time, times):
+        rows = CYL * 8 * times
+        north_out = dot(vis[0:rows], north[...]).reshape(CYL, 8 * times, 2 * NSB)
+        for t in range(times):
             one = north_out[:, 8 * t : 8 * t + 8, :].reshape(CYL * 8, 2 * NSB)
             one = jnp.concatenate([one[:, :NSB], one[:, NSB:]], 0).astype(bf16)
             beams = dot(east_t[...], one)
-            first = pl.multiple_of(q * 16 + t * 8, 8)
+            first = pl.multiple_of((time + t) * 8, 8)
             seen = refs[:, pl.ds(first, 8)].reshape(2 * 8 * EWB, NSB).astype(f32)
             resid = ((beams - seen).reshape(16, EWB, NSB) * weight_ref[...][None]).reshape(2 * 8 * EWB, NSB)
             adj = dot(east_adj[...], resid.astype(bf16)).astype(bf16)
             gfield[128 * t : 128 * (t + 1), 0:NSB] = adj[0:128]
             gfield[128 * t : 128 * (t + 1), NSB:] = adj[128:256]
-        field = dot(gfield[...], north_adj[...])
-        here = vis[...].astype(f32).reshape(CYL, 16, 2 * NSF)
-        for t in range(2):
+        field = dot(gfield[0:rows], north_adj[...])
+        here = vis[0:rows].astype(f32).reshape(CYL, 8 * times, 2 * NSF)
+        for t in range(times):
             f = field[128 * t : 128 * (t + 1)].reshape(CYL, 8, 2 * NSF)
             s = here[:, 8 * t : 8 * t + 8, :]
             torque = f[:, :, :NSF] * s[:, :, NSF:] - f[:, :, NSF:] * s[:, :, :NSF]
-            acc[...] += torque * keep[2 * q + t][None]
+            acc[...] += torque * keep[time + t][None]
+
+    def pair_step(i, _):
+        time = 2 * i
+        arrived(time)
+        gather_pair(time)
+        gradient(time, 2)
         return 0
 
-    lax.fori_loop(0, CHUNKS, chunk, 0)
+    def one_step(time, _):
+        arrived(time)
+        gather_one(time)
+        gradient(time, 1)
+        return 0
+
+    lax.fori_loop(0, 3, pair_step, 0)
+    lax.fori_loop(6, 8, one_step, 0)
 
     def over_chans(x):
         x = x + pltpu.roll(x, 4, 0)
@@ -271,8 +315,9 @@
         return 0
 
     lax.fori_loop(0, 15, send_total, 0)
-    for q in range(CHUNKS):
-        pltpu.make_async_copy(sky.at[q, pl.ds(0, FEED - 1)], sky.at[q, pl.ds(0, FEED - 1)], send_sem.at[q]).wait()
+    for m, (first, last) in enumerate(MESSAGES):
+        some = sky.at[0 : FEED - 1, first:last]
+        pltpu.make_async_copy(some, some, send_sem.at[m]).wait()
     some = piece.at[pl.ds(0, FEED - 1)]
     pltpu.make_async_copy(some, some, sum_sem.at[1]).wait()
     pltpu.make_async_copy(total_in, total_in, sum_sem.at[2]).wait()
@@ -312,8 +357,8 @@
             pltpu.VMEM((256, 512), bf16),
             pltpu.VMEM((256, 1024), bf16),
             pltpu.VMEM((1024, 256), bf16),
-            pltpu.VMEM((CHUNKS, FEED, 32, 128), bf16),
-            pltpu.VMEM((CHUNKS, FEED, 32, 128), bf16),
+            pltpu.VMEM((FEED, 8, 2, 8, 128), bf16),
+            pltpu.VMEM((FEED, 8, 2, 8, 128), bf16),
             pltpu.VMEM((2 * NSF, 2 * NSB), bf16),
             pltpu.VMEM((2 * NSB, 2 * NSF), bf16),
             pltpu.VMEM((8, 8, NSF), f32),
@@ -327,8 +372,8 @@
             pltpu.VMEM((4, 128), f32),
             pltpu.VMEM((16, 4, 128), f32),
             pltpu.SemaphoreType.DMA((11,)),
-            pltpu.SemaphoreType.DMA((CHUNKS,)),
-            pltpu.SemaphoreType.DMA((CHUNKS,)),
+            pltpu.SemaphoreType.DMA((len(MESSAGES),)),
+            pltpu.SemaphoreType.DMA((len(MESSAGES),)),
             pltpu.SemaphoreType.DMA((4,)),
         ],
         compiler_params=pltpu.CompilerParams(

time: 56.7 us -> 56.8 us (level)
  no operation moved by 1% of the time
where the time goes in v3:
time: 56.8 us; the launch traced here: 56.7 us
  Pallas kernels  54.9 us (97%)
  local copies, waits for them, and re-layouts  1.13 us (2%)
  between operations  0.64 us (1%)
    pallas_call x1, Pallas kernels, shards(): pl.pallas_call(kernel, out_shape=jax.ShapeDtypeStruct((4, 128), f32), in_...  54.9 us

profile of v3, /device:TPU:1, one launch (start us, length us, event | category | flops | bytes accessed | tf_op | source)
XLA Modules:
  0.0 56.7 jit_solution(15396739849080279156)
XLA Ops:
  0.6 54.9 %shard_map.122 = f32[4,128]{1,0:T(4,128)S(1)} custom-call(bf16[2,32,4,16,128]{4,3,2,1,0:T(8,128)(2,1)} %bitcast.5, bf16[2,64,32,512]{3,2,1,0:T(8,128)(2,1)} %bitcast.4, f32[32,512]{1,0:T(8,128)} %weight_hbm.1, f32[2,128]{1,0:T(2,128)} %delays_hbm.1, f32[2,16]{1,0:T(2,128)} %band_hbm.1, s32[4,256]{1,0:T(4,128)} %bitcast.6, s32[1,256]{1,0:T(1,128)} %bitcast.7, ...), custom_call_target="tpu_custom_call" | custom-call | tf_op jit(solution)/shard_map/pallas_call | solution.py:343
  55.5 0.6 slice.7
  56.1 0.6 slice.6
